TPU v7x, 512 devices: a whole 4x8x8 slice. The times are simulated.
512 devices in a mesh: leaf: 128 (over z, y, core), rhs: 4 (over x).
Axes of the slice: x: 4, y: 8, z: 8, core: 2. Of those that a mesh axis runs over, the one named last changes fastest.
Arguments:
- potential: float32 [128, 1048576], P('rhs', 'leaf'), may hold values from -6 to 6
- geometry: float32 [4, 1048576], P(None, 'leaf'), as said below
- near_count: int32 [4096], P('leaf'), may hold values from 3 to 12, as said below
- near_offset: int32 [4096, 12], P('leaf'), may hold values from -6 to 6, as said below
- far_offset: int32 [4096, 4], P('leaf'), may hold values from -8 to 8, as said below
- col_basis: bfloat16 [4096, 256, 64], P('leaf'), may hold values from -0.375 to 0.375
- row_basis: bfloat16 [4096, 256, 64], P('leaf'), may hold values from -0.5 to 0.5
- leaf_up: bfloat16 [4096, 64, 64], P('leaf'), may hold values from -0.125 to 0.125
- leaf_down: bfloat16 [4096, 64, 64], P('leaf'), may hold values from -0.75 to 0.75
- leaf_coupling: bfloat16 [4096, 4, 64, 64], P('leaf'), may hold values from -0.375 to 0.375
- up_transfer: bfloat16 [2, 64, 64], replicated, may hold values from -0.5 to 0.5
- down_transfer: bfloat16 [2, 64, 64], replicated, may hold values from -0.75 to 0.75
- sibling_coupling: bfloat16 [2, 64, 64], replicated, may hold values from -0.375 to 0.375
Outputs:
- field: float32 [128, 1048576], P('rhs', 'leaf')
Inputs may be any that keep to these rules, and one draw needn't show every extreme that they name: `geometry`: rows 0 to 2 are panel centroids, row 3 panel areas between 0.005 and 0.05. Each leaf cluster uses slots 0 to near_count - 1; some cluster uses all 12. `near_offset`: slot 0 of every cluster is the cluster itself (offset 0), slot 1 holds a positive offset and slot 2 a negative one; the other slots of a cluster hold distinct nonzero offsets. `far_offset`: every offset has magnitude above 6; the offsets of one cluster are distinct.
All inputs are finite; a program needn't handle non-finite values.
Results may differ from a plain program's by a relative error of at most 0.007.
Values may be sent and summed in bfloat16 or wider, within the bound.
No kernel may reach another device: no remote copies, remote signals or barrier semaphores. Data moves between devices by JAX's collectives and lax.ppermute only.
A program may use at most 64 MiB of HBM per device.

v0:
```python
import math
import jax
import jax.numpy as jnp
from jax import lax
from jax.sharding import PartitionSpec as P

NNEAR = 12
NWIN = 6
FWIN = 8


def with_halo(value, sides, width):
    for axis, dim in sides:
        devices, length = (lax.axis_size(axis), value.shape[dim])
        up = [(i, (i + 1) % devices) for i in range(devices - 1)]
        down = [(j, i) for i, j in up]
        last = lax.slice_in_dim(value, length - width, length, axis=dim)
        first = lax.slice_in_dim(value, 0, width, axis=dim)
        before = lax.ppermute(last, axis, up)
        after = lax.ppermute(first, axis, down)
        value = jnp.concatenate([before, value, after], axis=dim)
    return value


def from_partner(value, axis, apart):
    return lax.ppermute(value, axis, [(i, i ^ 1 << apart) for i in range(lax.axis_size(axis))])


def kernel_entries(target_geometry, source_geometry):
    squared = (target_geometry[0][:, :, None] - source_geometry[0][:, None, :]) ** 2
    squared = squared + (target_geometry[1][:, :, None] - source_geometry[1][:, None, :]) ** 2
    squared = squared + (target_geometry[2][:, :, None] - source_geometry[2][:, None, :]) ** 2
    spread = (target_geometry[3][:, :, None] + source_geometry[3][:, None, :]) / math.pi
    return source_geometry[3][:, None, :] / jnp.sqrt(squared + spread)


def select_side(table, side_bit):
    return lax.dynamic_index_in_dim(table, side_bit, 0, keepdims=False)


def per_device(
    potential,
    geometry,
    near_count,
    near_offset,
    far_offset,
    col_basis,
    row_basis,
    leaf_up,
    leaf_down,
    leaf_coupling,
    up_transfer,
    down_transfer,
    sibling_coupling,
):
    rows_here = potential.shape[0]
    clusters = near_count.shape[0]
    panels = col_basis.shape[1]
    basis_rank = col_basis.shape[2]
    partners_count = far_offset.shape[1]
    column_parts = lax.axis_size("rhs")
    per_part = clusters // column_parts
    first_local = lax.axis_index("rhs") * per_part
    window_width = per_part + 2 * NWIN
    stacked = jnp.concatenate([potential, geometry], axis=0)
    extended = with_halo(stacked, (("leaf", 1),), NWIN * panels)
    wide_rows = extended.shape[1] // panels
    value_rows = extended[:rows_here].astype(jnp.bfloat16)
    sources = lax.all_gather(value_rows, "rhs", axis=0, tiled=True)
    sources = sources.reshape(rows_here * column_parts, wide_rows, panels)
    all_rows = sources.shape[0]
    wide_geometry = extended[rows_here:].reshape(4, wide_rows, panels)
    local_geometry = lax.dynamic_slice_in_dim(wide_geometry, first_local, window_width, 1)
    target_geometry = local_geometry[:, NWIN : NWIN + per_part]
    live_counts = lax.dynamic_slice_in_dim(near_count, first_local, per_part, 0)
    offsets = lax.dynamic_slice_in_dim(near_offset, first_local, per_part, 0)
    own_clusters = NWIN + jnp.arange(per_part, dtype=jnp.int32)

    def add_slot(slot_index, running):
        shift_now = lax.dynamic_index_in_dim(offsets, slot_index, 1, keepdims=False)
        window_index = own_clusters + shift_now
        source_geometry = jnp.take(local_geometry, window_index, axis=1)
        source_values = jnp.take(sources, window_index + first_local, axis=1)
        live_mask = (slot_index < live_counts).astype(jnp.float32)
        near_block = (
            kernel_entries(target_geometry, source_geometry) * live_mask[:, None, None]
        ).astype(jnp.bfloat16)
        return running + jnp.einsum(
            "rcs,cts->rct", source_values, near_block, preferred_element_type=jnp.float32
        )

    start_sum = jnp.zeros((all_rows, per_part, panels), jnp.float32)
    near_part = lax.fori_loop(0, NNEAR, add_slot, start_sum)
    near_field = lax.all_to_all(
        near_part.reshape(all_rows, per_part * panels).astype(jnp.bfloat16),
        "rhs",
        split_axis=0,
        concat_axis=1,
        tiled=True,
    ).astype(jnp.float32)
    own_values = potential.astype(jnp.bfloat16).reshape(rows_here, clusters, panels)
    coefficients = jnp.einsum(
        "rcp,cpk->rck", own_values, col_basis, preferred_element_type=jnp.float32
    ).astype(jnp.bfloat16)
    rim_coefs = with_halo(
        coefficients.reshape(rows_here, clusters * basis_rank), (("leaf", 1),), FWIN * basis_rank
    )
    rim_coefs = rim_coefs.reshape(rows_here, clusters + 2 * FWIN, basis_rank)
    partner_index = jnp.arange(clusters, dtype=jnp.int32)[:, None] + FWIN + far_offset
    partners = jnp.take(rim_coefs, partner_index.reshape(-1), axis=1).reshape(
        rows_here, clusters, partners_count, basis_rank
    )
    leaf_far = jnp.einsum(
        "rcmk,cmkj->rcj", partners, leaf_coupling, preferred_element_type=jnp.float32
    )
    device_coef = jnp.einsum(
        "rck,ckj->rj", coefficients, leaf_up, preferred_element_type=jnp.float32
    ).astype(jnp.bfloat16)
    levels = lax.axis_size("leaf").bit_length() - 1
    device_index = lax.axis_index("leaf")
    couplings = []
    side_bits = []
    current = device_coef
    for tree_level in range(levels):
        side_bit = device_index // 2**tree_level % 2
        sibling = from_partner(current, "leaf", tree_level)
        couplings.append(
            jnp.dot(
                sibling, select_side(sibling_coupling, side_bit), preferred_element_type=jnp.float32
            )
        )
        side_bits.append(side_bit)
        if tree_level + 1 < levels:
            upward = jnp.dot(
                current, select_side(up_transfer, side_bit), preferred_element_type=jnp.float32
            )
            upward = upward + jnp.dot(
                sibling, select_side(up_transfer, 1 - side_bit), preferred_element_type=jnp.float32
            )
            current = upward.astype(jnp.bfloat16)
    local_sum = jnp.zeros((rows_here, basis_rank), jnp.float32)
    for tree_level in reversed(range(levels)):
        step_down = select_side(down_transfer, side_bits[tree_level]).astype(jnp.float32)
        local_sum = couplings[tree_level] + jnp.dot(
            local_sum, step_down, precision=lax.Precision.HIGHEST
        )
    leaf_local = leaf_far + jnp.einsum(
        "rk,ckj->rcj", local_sum, leaf_down.astype(jnp.float32), precision=lax.Precision.HIGHEST
    )
    leaf_local = leaf_local.astype(jnp.bfloat16)
    far_field = jnp.einsum(
        "rck,cpk->rcp", leaf_local, row_basis, preferred_element_type=jnp.float32
    )
    return near_field + far_field.reshape(rows_here, clusters * panels)


def solution(mesh):
    placed = (
        P("rhs", "leaf"),
        P(None, "leaf"),
        P("leaf"),
        P("leaf", None),
        P("leaf", None),
        P("leaf", None, None),
        P("leaf", None, None),
        P("leaf", None, None),
        P("leaf", None, None),
        P("leaf", None, None, None),
        P(),
        P(),
        P(),
    )
    return jax.shard_map(
        per_device, mesh=mesh, in_specs=placed, out_specs=P("rhs", "leaf"), check_vma=False
    )
```

profile of v0, /device:TPU:1, one launch (start us, length us, event | category | flops | bytes accessed | tf_op | source)
XLA Modules:
  0.0 244.2 jit_solution(15858377557532260188)
XLA Ops:
  9.3 8.8 %collective-permute-start.4 = (bf16[32,64]{1,0:T(8,128)(2,1)S(1)}, bf16[32,64]{1,0:T(8,128)(2,1)S(1)}, u32[]{:S(2)}, u32[]{:S(2)}) collective-permute-start(bf16[32,64]{1,0:T(8,128)(2,1)S(1)} %fusion.23), channel_id=1, source_target_pairs={{0,4},{4,0},{8,12},{12,8},{16,20},{20,16},{24,28},{28,24},{32,36},... | collective-permute-start | bytes 12296 | tf_op jit(solution)/shard_map/ppermute | solution.py:26
  24.1 3.0 %collective-permute-start.3 = (bf16[32,512]{1,0:T(8,128)(2,1)}, bf16[32,512]{1,0:T(8,128)(2,1)}, u32[]{:S(2)}, u32[]{:S(2)}) collective-permute-start(bf16[32,512]{1,0:T(8,128)(2,1)} %get-tuple-element.251), channel_id=1, source_target_pairs={{4,0},{8,4},{12,8},{16,12},{20,16},{24,20},{28,24},{32,28},{36,32}... | collective-permute-start | bytes 98312 | tf_op jit(solution)/shard_map/ppermute | solution.py:20
  43.2 3.2 %collective-permute-done.6 = bf16[32,64]{1,0:T(8,128)(2,1)S(1)} collective-permute-done((bf16[32,64]{1,0:T(8,128)(2,1)S(1)}, bf16[32,64]{1,0:T(8,128)(2,1)S(1)}, u32[]{:S(2)}, u32[]{:S(2)}) %collective-permute-start.6) | collective-permute-done | bytes 4128 | tf_op jit(solution)/shard_map/ppermute | solution.py:26
  49.1 5.7 %collective-permute-done.7 = bf16[32,64]{1,0:T(8,128)(2,1)S(1)} collective-permute-done((bf16[32,64]{1,0:T(8,128)(2,1)S(1)}, bf16[32,64]{1,0:T(8,128)(2,1)S(1)}, u32[]{:S(2)}, u32[]{:S(2)}) %collective-permute-start.7) | collective-permute-done | bytes 4128 | tf_op jit(solution)/shard_map/ppermute | solution.py:26
  64.1 5.0 %collective-permute-start.9 = (bf16[32,64]{1,0:T(8,128)(2,1)S(1)}, bf16[32,64]{1,0:T(8,128)(2,1)S(1)}, u32[]{:S(2)}, u32[]{:S(2)}) collective-permute-start(bf16[32,64]{1,0:T(8,128)(2,1)S(1)} %fusion.28), channel_id=1, source_target_pairs={{0,128},{4,132},{8,136},{12,140},{16,144},{20,148},{24,152},{28,15... | collective-permute-start | bytes 12296 | tf_op jit(solution)/shard_map/ppermute | solution.py:26
  70.3 8.3 %collective-permute-start.10 = (bf16[32,64]{1,0:T(8,128)(2,1)S(1)}, bf16[32,64]{1,0:T(8,128)(2,1)S(1)}, u32[]{:S(2)}, u32[]{:S(2)}) collective-permute-start(bf16[32,64]{1,0:T(8,128)(2,1)S(1)} %fusion.29), channel_id=1, source_target_pairs={{0,256},{4,260},{8,264},{12,268},{16,272},{20,276},{24,280},{28,28... | collective-permute-start | bytes 12296 | tf_op jit(solution)/shard_map/ppermute | solution.py:26
  91.8 21.3 %all-gather.2.cloned.1.call-done = bf16[128,11264]{1,0:T(8,128)(2,1)} async-done(((bf16[32,11264]{1,0:T(8,128)(2,1)}), bf16[128,11264]{1,0:T(8,128)(2,1)}) %all-gather.2.cloned.1.call-update) | async-done | bytes 2883600 | tf_op jit(solution)/shard_map/all_gather | solution.py:69
  113.1 4.6 %copy.43 = bf16[128,11264]{0,1:T(8,128)(2,1)} copy(bf16[128,11264]{1,0:T(8,128)(2,1)} %all-gather.2.cloned.1.call-done) | data formatting | bytes 5767168 | tf_op jit(solution)/shard_map/all_gather | solution.py:69
  117.6 4.6 %copy.45 = bf16[128,44,256]{2,0,1:T(8,128)(2,1)} copy(bf16[128,44,256]{0,2,1:T(8,128)(2,1)} %bitcast.197) | data formatting | bytes 5767168
  122.2 96.9 %while.14 = (s32[]{:T(128)}, f32[128,8,256]{0,2,1:T(8,128)}, s32[8,12]{0,1:T(8,128)}, f32[4,20,256]{2,0,1:T(4,128)S(1)}, f32[4,8,256]{2,1,0:T(8,128)S(1)}, /*ind...) while((s32[]{:T(128)}, f32[128,8,256]{0,2,1:T(8,128)}, ...), condition=%wide.region_1.2_spmd.clone, body=%wide.region_0.1_spmd.clone.sunk | while | flops 142354592 | bytes 4071995 | solution.py:93
  126.1 2.9 %fusion.174 = f32[128,8,256]{0,2,1:T(8,128)} fusion(f32[128,8,256]{0,2,1:T(8,128)} %get-tuple-element.342, f32[8]{0:T(128)S(1)} %compare_convert_fusion.2, f32[8,256]{1,0:T(8,128)S(1)} %get-tuple-element.316, f32[8,256]{1,0:T(8,128)S(1)} %get-tuple-element.320, f32[8,256]{1,0:T(8,128)S(1)} %get-tuple-element.321, ...), kind=kOutput, calls=%fused_computation.6.clone.1 | convolution fusion | flops 142344192 | bytes 2687017 | tf_op jit(solution)/shard_map/while/body/eval_jaxpr/rcs,cts->rct/dot_general | solution.py:88
  132.9 4.3 %fusion.174 = f32[128,8,256]{0,2,1:T(8,128)} fusion(f32[128,8,256]{0,2,1:T(8,128)} %get-tuple-element.342, f32[8]{0:T(128)S(1)} %compare_convert_fusion.2, f32[8,256]{1,0:T(8,128)S(1)} %get-tuple-element.316, f32[8,256]{1,0:T(8,128)S(1)} %get-tuple-element.320, f32[8,256]{1,0:T(8,128)S(1)} %get-tuple-element.321, ...), kind=kOutput, calls=%fused_computation.6.clone.1 | convolution fusion | flops 142344192 | bytes 2687017 | tf_op jit(solution)/shard_map/while/body/eval_jaxpr/rcs,cts->rct/dot_general | solution.py:88
  141.1 4.3 %fusion.174 = f32[128,8,256]{0,2,1:T(8,128)} fusion(f32[128,8,256]{0,2,1:T(8,128)} %get-tuple-element.342, f32[8]{0:T(128)S(1)} %compare_convert_fusion.2, f32[8,256]{1,0:T(8,128)S(1)} %get-tuple-element.316, f32[8,256]{1,0:T(8,128)S(1)} %get-tuple-element.320, f32[8,256]{1,0:T(8,128)S(1)} %get-tuple-element.321, ...), kind=kOutput, calls=%fused_computation.6.clone.1 | convolution fusion | flops 142344192 | bytes 2687017 | tf_op jit(solution)/shard_map/while/body/eval_jaxpr/rcs,cts->rct/dot_general | solution.py:88
  149.3 4.3 %fusion.174 = f32[128,8,256]{0,2,1:T(8,128)} fusion(f32[128,8,256]{0,2,1:T(8,128)} %get-tuple-element.342, f32[8]{0:T(128)S(1)} %compare_convert_fusion.2, f32[8,256]{1,0:T(8,128)S(1)} %get-tuple-element.316, f32[8,256]{1,0:T(8,128)S(1)} %get-tuple-element.320, f32[8,256]{1,0:T(8,128)S(1)} %get-tuple-element.321, ...), kind=kOutput, calls=%fused_computation.6.clone.1 | convolution fusion | flops 142344192 | bytes 2687017 | tf_op jit(solution)/shard_map/while/body/eval_jaxpr/rcs,cts->rct/dot_general | solution.py:88
  157.4 4.3 %fusion.174 = f32[128,8,256]{0,2,1:T(8,128)} fusion(f32[128,8,256]{0,2,1:T(8,128)} %get-tuple-element.342, f32[8]{0:T(128)S(1)} %compare_convert_fusion.2, f32[8,256]{1,0:T(8,128)S(1)} %get-tuple-element.316, f32[8,256]{1,0:T(8,128)S(1)} %get-tuple-element.320, f32[8,256]{1,0:T(8,128)S(1)} %get-tuple-element.321, ...), kind=kOutput, calls=%fused_computation.6.clone.1 | convolution fusion | flops 142344192 | bytes 2687017 | tf_op jit(solution)/shard_map/while/body/eval_jaxpr/rcs,cts->rct/dot_general | solution.py:88
  165.6 4.3 %fusion.174 = f32[128,8,256]{0,2,1:T(8,128)} fusion(f32[128,8,256]{0,2,1:T(8,128)} %get-tuple-element.342, f32[8]{0:T(128)S(1)} %compare_convert_fusion.2, f32[8,256]{1,0:T(8,128)S(1)} %get-tuple-element.316, f32[8,256]{1,0:T(8,128)S(1)} %get-tuple-element.320, f32[8,256]{1,0:T(8,128)S(1)} %get-tuple-element.321, ...), kind=kOutput, calls=%fused_computation.6.clone.1 | convolution fusion | flops 142344192 | bytes 2687017 | tf_op jit(solution)/shard_map/while/body/eval_jaxpr/rcs,cts->rct/dot_general | solution.py:88
  173.8 4.3 %fusion.174 = f32[128,8,256]{0,2,1:T(8,128)} fusion(f32[128,8,256]{0,2,1:T(8,128)} %get-tuple-element.342, f32[8]{0:T(128)S(1)} %compare_convert_fusion.2, f32[8,256]{1,0:T(8,128)S(1)} %get-tuple-element.316, f32[8,256]{1,0:T(8,128)S(1)} %get-tuple-element.320, f32[8,256]{1,0:T(8,128)S(1)} %get-tuple-element.321, ...), kind=kOutput, calls=%fused_computation.6.clone.1 | convolution fusion | flops 142344192 | bytes 2687017 | tf_op jit(solution)/shard_map/while/body/eval_jaxpr/rcs,cts->rct/dot_general | solution.py:88
  182.0 4.3 %fusion.174 = f32[128,8,256]{0,2,1:T(8,128)} fusion(f32[128,8,256]{0,2,1:T(8,128)} %get-tuple-element.342, f32[8]{0:T(128)S(1)} %compare_convert_fusion.2, f32[8,256]{1,0:T(8,128)S(1)} %get-tuple-element.316, f32[8,256]{1,0:T(8,128)S(1)} %get-tuple-element.320, f32[8,256]{1,0:T(8,128)S(1)} %get-tuple-element.321, ...), kind=kOutput, calls=%fused_computation.6.clone.1 | convolution fusion | flops 142344192 | bytes 2687017 | tf_op jit(solution)/shard_map/while/body/eval_jaxpr/rcs,cts->rct/dot_general | solution.py:88
  190.2 4.3 %fusion.174 = f32[128,8,256]{0,2,1:T(8,128)} fusion(f32[128,8,256]{0,2,1:T(8,128)} %get-tuple-element.342, f32[8]{0:T(128)S(1)} %compare_convert_fusion.2, f32[8,256]{1,0:T(8,128)S(1)} %get-tuple-element.316, f32[8,256]{1,0:T(8,128)S(1)} %get-tuple-element.320, f32[8,256]{1,0:T(8,128)S(1)} %get-tuple-element.321, ...), kind=kOutput, calls=%fused_computation.6.clone.1 | convolution fusion | flops 142344192 | bytes 2687017 | tf_op jit(solution)/shard_map/while/body/eval_jaxpr/rcs,cts->rct/dot_general | solution.py:88
  198.4 4.3 %fusion.174 = f32[128,8,256]{0,2,1:T(8,128)} fusion(f32[128,8,256]{0,2,1:T(8,128)} %get-tuple-element.342, f32[8]{0:T(128)S(1)} %compare_convert_fusion.2, f32[8,256]{1,0:T(8,128)S(1)} %get-tuple-element.316, f32[8,256]{1,0:T(8,128)S(1)} %get-tuple-element.320, f32[8,256]{1,0:T(8,128)S(1)} %get-tuple-element.321, ...), kind=kOutput, calls=%fused_computation.6.clone.1 | convolution fusion | flops 142344192 | bytes 2687017 | tf_op jit(solution)/shard_map/while/body/eval_jaxpr/rcs,cts->rct/dot_general | solution.py:88
  206.6 4.3 %fusion.174 = f32[128,8,256]{0,2,1:T(8,128)} fusion(f32[128,8,256]{0,2,1:T(8,128)} %get-tuple-element.342, f32[8]{0:T(128)S(1)} %compare_convert_fusion.2, f32[8,256]{1,0:T(8,128)S(1)} %get-tuple-element.316, f32[8,256]{1,0:T(8,128)S(1)} %get-tuple-element.320, f32[8,256]{1,0:T(8,128)S(1)} %get-tuple-element.321, ...), kind=kOutput, calls=%fused_computation.6.clone.1 | convolution fusion | flops 142344192 | bytes 2687017 | tf_op jit(solution)/shard_map/while/body/eval_jaxpr/rcs,cts->rct/dot_general | solution.py:88
  214.8 4.3 %fusion.174 = f32[128,8,256]{0,2,1:T(8,128)} fusion(f32[128,8,256]{0,2,1:T(8,128)} %get-tuple-element.342, f32[8]{0:T(128)S(1)} %compare_convert_fusion.2, f32[8,256]{1,0:T(8,128)S(1)} %get-tuple-element.316, f32[8,256]{1,0:T(8,128)S(1)} %get-tuple-element.320, f32[8,256]{1,0:T(8,128)S(1)} %get-tuple-element.321, ...), kind=kOutput, calls=%fused_computation.6.clone.1 | convolution fusion | flops 142344192 | bytes 2687017 | tf_op jit(solution)/shard_map/while/body/eval_jaxpr/rcs,cts->rct/dot_general | solution.py:88
  221.9 4.1 %all-to-all-start = ((bf16[4,32,2048]{2,1,0:T(8,128)(2,1)}), bf16[4,32,2048]{2,1,0:T(8,128)(2,1)}, u32[]{:S(2)}, u32[]{:S(2)}) async-start(bf16[4,32,2048]{2,1,0:T(8,128)(2,1)} %convert_element_type.77), calls=%async_computation | async-start | bytes 1048576 | tf_op jit(solution)/shard_map/all_to_all | solution.py:94
  229.1 6.0 %all-to-all-done = bf16[4,32,2048]{2,1,0:T(8,128)(2,1)} async-done(((bf16[4,32,2048]{2,1,0:T(8,128)(2,1)}), bf16[4,32,2048]{2,1,0:T(8,128)(2,1)}, u32[]{:S(2)}, u32[]{:S(2)}) %all-to-all-start) | async-done | bytes 524320 | tf_op jit(solution)/shard_map/all_to_all | solution.py:94
  (269 shorter events, 104.4 us)
Async XLA Ops:
  6.5 80.3 %copy-start = (bf16[32,4,64,64]{3,2,1,0:T(8,128)(2,1)S(1)}, bf16[32,4,64,64]{3,2,1,0:T(8,128)(2,1)}, u32[]{:S(2)}) copy-start(bf16[32,4,64,64]{3,2,1,0:T(8,128)(2,1)} %param.24) | copy-start | bytes 3145732
  6.5 106.5 %all-gather.2.cloned.1.call-start = ((), (), s32[]{:S(2)}) async-start(), calls=%async_computation.1 | async-start | bytes 3604480 | tf_op jit(solution)/shard_map/all_gather | solution.py:69
  9.0 25.0 %copy-start.13 = (s32[32,4]{0,1:T(4,128)S(1)}, s32[32,4]{0,1:T(4,128)}, u32[]{:S(2)}) copy-start(s32[32,4]{0,1:T(4,128)} %param.19) | copy-start | bytes 1540
  9.0 26.3 %copy-start.2 = (bf16[2,64,64]{2,1,0:T(8,128)(2,1)S(1)}, bf16[2,64,64]{2,1,0:T(8,128)(2,1)}, u32[]{:S(2)}) copy-start(bf16[2,64,64]{2,1,0:T(8,128)(2,1)} %param.25) | copy-start | bytes 49156
  9.0 26.4 %copy-start.6 = (bf16[2,64,64]{2,1,0:T(8,128)(2,1)S(1)}, bf16[2,64,64]{2,1,0:T(8,128)(2,1)}, u32[]{:S(2)}) copy-start(bf16[2,64,64]{2,1,0:T(8,128)(2,1)} %param.26) | copy-start | bytes 49156
  9.0 26.5 %copy-start.12 = (s32[32,12]{0,1:T(8,128)S(1)}, s32[32,12]{0,1:T(8,128)}, u32[]{:S(2)}) copy-start(s32[32,12]{0,1:T(8,128)} %param.18) | copy-start | bytes 4612
  9.3 26.9 %collective-permute-start.4 = (bf16[32,64]{1,0:T(8,128)(2,1)S(1)}, bf16[32,64]{1,0:T(8,128)(2,1)S(1)}, u32[]{:S(2)}, u32[]{:S(2)}) collective-permute-start(bf16[32,64]{1,0:T(8,128)(2,1)S(1)} %fusion.23), channel_id=1, source_target_pairs={{0,4},{4,0},{8,12},{12,8},{16,20},{20,16},{24,28},{28,24},{32,36},... | collective-permute-start | bytes 12296 | tf_op jit(solution)/shard_map/ppermute | solution.py:26
  22.2 62.5 %collective-permute-start.2 = (bf16[32,512]{1,0:T(8,128)(2,1)}, bf16[32,512]{1,0:T(8,128)(2,1)}, u32[]{:S(2)}, u32[]{:S(2)}) collective-permute-start(bf16[32,512]{1,0:T(8,128)(2,1)} %get-tuple-element.250), channel_id=1, source_target_pairs={{0,4},{4,8},{8,12},{12,16},{16,20},{20,24},{24,28},{28,32},{32,36}... | collective-permute-start | bytes 98312 | tf_op jit(solution)/shard_map/ppermute | solution.py:19
  24.1 60.6 %collective-permute-start.3 = (bf16[32,512]{1,0:T(8,128)(2,1)}, bf16[32,512]{1,0:T(8,128)(2,1)}, u32[]{:S(2)}, u32[]{:S(2)}) collective-permute-start(bf16[32,512]{1,0:T(8,128)(2,1)} %get-tuple-element.251), channel_id=1, source_target_pairs={{4,0},{8,4},{12,8},{16,12},{20,16},{24,20},{28,24},{32,28},{36,32}... | collective-permute-start | bytes 98312 | tf_op jit(solution)/shard_map/ppermute | solution.py:20
  28.8 29.5 %collective-permute-start = (f32[36,1536]{1,0:T(8,128)}, f32[36,1536]{1,0:T(8,128)}, u32[]{:S(2)}, u32[]{:S(2)}) collective-permute-start(f32[36,1536]{1,0:T(8,128)} %get-tuple-element.246), channel_id=1, source_target_pairs={{0,4},{4,8},{8,12},{12,16},{16,20},{20,24},{24,28},{28,32},{32,36}... | collective-permute-start | bytes 663560 | tf_op jit(solution)/shard_map/ppermute | solution.py:19
  31.4 27.0 %collective-permute-start.1 = (f32[36,1536]{1,0:T(8,128)}, f32[36,1536]{1,0:T(8,128)}, u32[]{:S(2)}, u32[]{:S(2)}) collective-permute-start(f32[36,1536]{1,0:T(8,128)} %get-tuple-element.247), channel_id=1, source_target_pairs={{4,0},{8,4},{12,8},{16,12},{20,16},{24,20},{28,24},{32,28},{36,32}... | collective-permute-start | bytes 663560 | tf_op jit(solution)/shard_map/ppermute | solution.py:20
  36.2 21.3 %copy-start.8 = (bf16[32,64]{1,0:T(8,128)(2,1)}, bf16[32,64]{1,0:T(8,128)(2,1)S(1)}, u32[]{:S(2)}) copy-start(bf16[32,64]{1,0:T(8,128)(2,1)S(1)} %collective-permute-done.4) | copy-start | bytes 12292
  36.3 4.7 %collective-permute-start.5 = (bf16[32,64]{1,0:T(8,128)(2,1)S(1)}, bf16[32,64]{1,0:T(8,128)(2,1)S(1)}, u32[]{:S(2)}, u32[]{:S(2)}) collective-permute-start(bf16[32,64]{1,0:T(8,128)(2,1)S(1)} %fusion.24), channel_id=1, source_target_pairs={{0,8},{4,12},{8,0},{12,4},{16,24},{20,28},{24,16},{28,20},{32,40},... | collective-permute-start | bytes 12296 | tf_op jit(solution)/shard_map/ppermute | solution.py:26
  41.1 5.3 %collective-permute-start.6 = (bf16[32,64]{1,0:T(8,128)(2,1)S(1)}, bf16[32,64]{1,0:T(8,128)(2,1)S(1)}, u32[]{:S(2)}, u32[]{:S(2)}) collective-permute-start(bf16[32,64]{1,0:T(8,128)(2,1)S(1)} %fusion.25), channel_id=1, source_target_pairs={{0,16},{4,20},{8,24},{12,28},{16,0},{20,4},{24,8},{28,12},{32,48},... | collective-permute-start | bytes 12296 | tf_op jit(solution)/shard_map/ppermute | solution.py:26
  46.6 8.3 %collective-permute-start.7 = (bf16[32,64]{1,0:T(8,128)(2,1)S(1)}, bf16[32,64]{1,0:T(8,128)(2,1)S(1)}, u32[]{:S(2)}, u32[]{:S(2)}) collective-permute-start(bf16[32,64]{1,0:T(8,128)(2,1)S(1)} %fusion.26), channel_id=1, source_target_pairs={{0,32},{4,36},{8,40},{12,44},{16,48},{20,52},{24,56},{28,60},{32,0... | collective-permute-start | bytes 12296 | tf_op jit(solution)/shard_map/ppermute | solution.py:26
  55.6 7.6 %collective-permute-start.8 = (bf16[32,64]{1,0:T(8,128)(2,1)}, bf16[32,64]{1,0:T(8,128)(2,1)}, u32[]{:S(2)}, u32[]{:S(2)}) collective-permute-start(bf16[32,64]{1,0:T(8,128)(2,1)} %fusion.27), channel_id=1, source_target_pairs={{0,64},{4,68},{8,72},{12,76},{16,80},{20,84},{24,88},{28,92},{32,9... | collective-permute-start | bytes 12296 | tf_op jit(solution)/shard_map/ppermute | solution.py:26
  58.4 23.8 %copy-start.7 = (bf16[2,64,64]{2,1,0:T(8,128)(2,1)S(1)}, bf16[2,64,64]{2,1,0:T(8,128)(2,1)}, u32[]{:S(2)}) copy-start(bf16[2,64,64]{2,1,0:T(8,128)(2,1)} %param.27) | copy-start | bytes 49156
  60.8 22.9 %copy-start.11 = (bf16[32,64]{1,0:T(8,128)(2,1)S(1)}, bf16[32,64]{1,0:T(8,128)(2,1)}, u32[]{:S(2)}) copy-start(bf16[32,64]{1,0:T(8,128)(2,1)} %copy-done.10) | copy-start | bytes 12292
  60.8 23.7 %copy-start.9 = (bf16[32,64]{1,0:T(8,128)(2,1)S(1)}, bf16[32,64]{1,0:T(8,128)(2,1)}, u32[]{:S(2)}) copy-start(bf16[32,64]{1,0:T(8,128)(2,1)} %copy-done.8) | copy-start | bytes 12292
  60.8 23.9 %copy-start.4 = (bf16[32,2048]{1,0:T(8,128)(2,1)S(1)}, bf16[32,2048]{1,0:T(8,128)(2,1)}, u32[]{:S(2)}) copy-start(bf16[32,2048]{1,0:T(8,128)(2,1)} %reshape.114) | copy-start | bytes 393220
  64.1 6.1 %collective-permute-start.9 = (bf16[32,64]{1,0:T(8,128)(2,1)S(1)}, bf16[32,64]{1,0:T(8,128)(2,1)S(1)}, u32[]{:S(2)}, u32[]{:S(2)}) collective-permute-start(bf16[32,64]{1,0:T(8,128)(2,1)S(1)} %fusion.28), channel_id=1, source_target_pairs={{0,128},{4,132},{8,136},{12,140},{16,144},{20,148},{24,152},{28,15... | collective-permute-start | bytes 12296 | tf_op jit(solution)/shard_map/ppermute | solution.py:26
  70.3 11.9 %collective-permute-start.10 = (bf16[32,64]{1,0:T(8,128)(2,1)S(1)}, bf16[32,64]{1,0:T(8,128)(2,1)S(1)}, u32[]{:S(2)}, u32[]{:S(2)}) collective-permute-start(bf16[32,64]{1,0:T(8,128)(2,1)S(1)} %fusion.29), channel_id=1, source_target_pairs={{0,256},{4,260},{8,264},{12,268},{16,272},{20,276},{24,280},{28,28... | collective-permute-start | bytes 12296 | tf_op jit(solution)/shard_map/ppermute | solution.py:26
  220.8 5.2 %copy-start.1 = (f32[32,32,64]{2,0,1:T(8,128)S(1)}, f32[32,32,64]{2,0,1:T(8,128)}, u32[]{:S(2)}) copy-start(f32[32,32,64]{2,0,1:T(8,128)} %convolution_bitcast_fusion.2) | copy-start | bytes 786436
  221.9 13.2 %all-to-all-start = ((bf16[4,32,2048]{2,1,0:T(8,128)(2,1)}), bf16[4,32,2048]{2,1,0:T(8,128)(2,1)}, u32[]{:S(2)}, u32[]{:S(2)}) async-start(bf16[4,32,2048]{2,1,0:T(8,128)(2,1)} %convert_element_type.77), calls=%async_computation | async-start | bytes 1048576 | tf_op jit(solution)/shard_map/all_to_all | solution.py:94
  (4 other events, 11.6 us)
Sparse Core Ops, SparseCore 0:
  63.3 49.6 all-gather.1
where the time goes:
time: 247 us; the launch traced here: 244 us
  local copies, waits for them, and re-layouts  62.7 us (25%)
  matrix products  62.2 us (25%)
  starting transfers between devices  44.3 us (18%)
  waiting for transfers between devices  39.9 us (16%)
  other arithmetic  20.4 us (8%)
  between operations  13.9 us (6%)
    dot_general x12, matrix products, add_slot(): jnp.einsum('rcs,cts->rct', source_values, near_block, preferred_element_t...  50.4 us
    ppermute x7, starting transfers between devices, from_partner(): lax.ppermute(value, axis, [(i, i ^ 1 << apart) for i in range(lax.axis_si...  30.3 us
    gather x12, local copies, waits for them, and re-layouts, add_slot(): source_values = jnp.take(sources, window_index + first_local, axis=1)  28.7 us
    all_gather x1, waiting for transfers between devices, per_device(): sources = lax.all_gather(value_rows, 'rhs', axis=0, tiled=True)  21.3 us
    ppermute x7, waiting for transfers between devices, from_partner(): lax.ppermute(value, axis, [(i, i ^ 1 << apart) for i in range(lax.axis_si...  12.5 us
    reduce_and x12, other arithmetic, add_slot(): source_values = jnp.take(sources, window_index + first_local, axis=1)  8.28 us
    gather x12, local copies, waits for them, and re-layouts, add_slot(): source_geometry = jnp.take(local_geometry, window_index, axis=1)  6.92 us
    all_to_all x1, waiting for transfers between devices, per_device(): lax.all_to_all(near_part.reshape(all_rows, per_part * panels).astype(jnp....  6.04 us
  transfers between devices with their start and end apart: 13, of which 6 were waited for; matrix products, arithmetic and copies ran while one was open for 13% of the time, Pallas kernels for 0%

commit v1 on v0

--- a/solution.py
+++ b/solution.py
@@ -7,6 +7,22 @@
 NNEAR = 12
 NWIN = 6
 FWIN = 8
+
+
+def collect(x, axis, dim):
+    ways, here, lap = (lax.axis_size(axis), lax.axis_index(axis), x.shape[dim])
+    shape = [n * ways if d == dim else n for d, n in enumerate(x.shape)]
+    full = lax.dynamic_update_slice_in_dim(jnp.zeros(shape, x.dtype), x, here * lap, axis=dim)
+    going_up = going_down = x
+    for far in range(1, ways // 2 + 1):
+        going_up = lax.ppermute(going_up, axis, [(d, (d + 1) % ways) for d in range(ways)])
+        full = lax.dynamic_update_slice_in_dim(full, going_up, (here - far) % ways * lap, axis=dim)
+        if 2 * far < ways:
+            going_down = lax.ppermute(going_down, axis, [(d, (d - 1) % ways) for d in range(ways)])
+            full = lax.dynamic_update_slice_in_dim(
+                full, going_down, (here + far) % ways * lap, axis=dim
+            )
+    return full
 
 
 def with_halo(value, sides, width):
@@ -66,7 +82,7 @@
     extended = with_halo(stacked, (("leaf", 1),), NWIN * panels)
     wide_rows = extended.shape[1] // panels
     value_rows = extended[:rows_here].astype(jnp.bfloat16)
-    sources = lax.all_gather(value_rows, "rhs", axis=0, tiled=True)
+    sources = collect(value_rows, "rhs", 0)
     sources = sources.reshape(rows_here * column_parts, wide_rows, panels)
     all_rows = sources.shape[0]
     wide_geometry = extended[rows_here:].reshape(4, wide_rows, panels)

time: 247 us -> 369 us (1.49)
  the two profiles are of different devices: /device:TPU:1 before, /device:TPU:56 now
where the time goes in v1:
time: 369 us; the launch traced here: 363 us
  local copies, waits for them, and re-layouts  191 us (52%)
  matrix products  63.3 us (17%)
  starting transfers between devices  58.3 us (16%)
  waiting for transfers between devices  30.3 us (8%)
  other arithmetic  19.3 us (5%)
    dynamic_update_slice x2, local copies, waits for them, and re-layouts, collect(): lax.dynamic_update_slice_in_dim(full, going_up, (here - far) % ways * lap...  61.8 us
    dot_general x12, matrix products, add_slot(): jnp.einsum('rcs,cts->rct', source_values, near_block, preferred_element_t...  50.4 us
    ppermute x7, starting transfers between devices, from_partner(): lax.ppermute(value, axis, [(i, i ^ 1 << apart) for i in range(lax.axis_si...  32.2 us
    dynamic_update_slice x1, local copies, waits for them, and re-layouts, collect(): lax.dynamic_update_slice_in_dim(full, going_down, (here + far) % ways * l...  30.9 us
    gather x12, local copies, waits for them, and re-layouts, add_slot(): source_values = jnp.take(sources, window_index + first_local, axis=1)  28.7 us
    dynamic_update_slice x1, local copies, waits for them, and re-layouts, collect(): lax.dynamic_update_slice_in_dim(jnp.zeros(shape, x.dtype), x, here * lap,...  26.3 us
    ppermute x7, waiting for transfers between devices, from_partner(): lax.ppermute(value, axis, [(i, i ^ 1 << apart) for i in range(lax.axis_si...  17.1 us
    reduce_and x12, other arithmetic, add_slot(): source_values = jnp.take(sources, window_index + first_local, axis=1)  8.35 us
  transfers between devices with their start and end apart: 15, of which 7 were waited for; matrix products, arithmetic and copies ran while one was open for 35% of the time, Pallas kernels for 0%

profile of v1, /device:TPU:56, one launch (start us, length us, event | category | flops | bytes accessed | tf_op | source)
XLA Modules:
  0.0 363.4 jit_solution(817704173546104913)
XLA Ops:
  20.8 5.8 %collective-permute-start.7 = (bf16[32,64]{1,0:T(8,128)(2,1)S(1)}, bf16[32,64]{1,0:T(8,128)(2,1)S(1)}, u32[]{:S(2)}, u32[]{:S(2)}) collective-permute-start(bf16[32,64]{1,0:T(8,128)(2,1)S(1)} %fusion.23), channel_id=1, source_target_pairs={{0,4},{4,0},{8,12},{12,8},{16,20},{20,16},{24,28},{28,24},{32,36},... | collective-permute-start | bytes 12296 | tf_op jit(solution)/shard_map/ppermute | solution.py:42
  36.8 4.4 %collective-permute-done.9 = bf16[32,64]{1,0:T(8,128)(2,1)S(1)} collective-permute-done((bf16[32,64]{1,0:T(8,128)(2,1)S(1)}, bf16[32,64]{1,0:T(8,128)(2,1)S(1)}, u32[]{:S(2)}, u32[]{:S(2)}) %collective-permute-start.9) | collective-permute-done | bytes 4128 | tf_op jit(solution)/shard_map/ppermute | solution.py:42
  44.5 6.3 %collective-permute-done.10 = bf16[32,64]{1,0:T(8,128)(2,1)S(1)} collective-permute-done((bf16[32,64]{1,0:T(8,128)(2,1)S(1)}, bf16[32,64]{1,0:T(8,128)(2,1)S(1)}, u32[]{:S(2)}, u32[]{:S(2)}) %collective-permute-start.10) | collective-permute-done | bytes 4128 | tf_op jit(solution)/shard_map/ppermute | solution.py:42
  56.9 8.5 %collective-permute-start.12 = (bf16[32,64]{1,0:T(8,128)(2,1)S(1)}, bf16[32,64]{1,0:T(8,128)(2,1)S(1)}, u32[]{:S(2)}, u32[]{:S(2)}) collective-permute-start(bf16[32,64]{1,0:T(8,128)(2,1)S(1)} %fusion.28), channel_id=1, source_target_pairs={{0,128},{4,132},{8,136},{12,140},{16,144},{20,148},{24,152},{28,15... | collective-permute-start | bytes 12296 | tf_op jit(solution)/shard_map/ppermute | solution.py:42
  67.8 6.9 %collective-permute-start.13 = (bf16[32,64]{1,0:T(8,128)(2,1)}, bf16[32,64]{1,0:T(8,128)(2,1)S(1)}, u32[]{:S(2)}, u32[]{:S(2)}) collective-permute-start(bf16[32,64]{1,0:T(8,128)(2,1)} %fusion.29), channel_id=1, source_target_pairs={{0,256},{4,260},{8,264},{12,268},{16,272},{20,276},{24,280},{28,28... | collective-permute-start | bytes 12296 | tf_op jit(solution)/shard_map/ppermute | solution.py:42
  92.8 8.0 %collective-permute-done.2 = bf16[32,11264]{1,0:T(8,128)(2,1)} collective-permute-done((bf16[32,11264]{1,0:T(8,128)(2,1)}, bf16[32,11264]{1,0:T(8,128)(2,1)}, u32[]{:S(2)}, u32[]{:S(2)}) %collective-permute-start.2) | collective-permute-done | bytes 720928 | tf_op jit(solution)/shard_map/ppermute | solution.py:18
  114.3 26.3 %dynamic_update_slice.12 = bf16[128,11264]{0,1:T(8,128)(2,1)} dynamic-update-slice(bf16[128,11264]{0,1:T(8,128)(2,1)} %broadcast_in_dim.64, bf16[32,11264]{0,1:T(8,128)(2,1)} %copy.59, s32[]{:T(128)S(6)} %select_n.206, s32[]{:T(128)} %constant.288.clone.1) | dynamic-update-slice | bytes 1441796 | tf_op jit(solution)/shard_map/dynamic_update_slice | solution.py:15
  144.4 30.9 %dynamic_update_slice.13 = bf16[128,11264]{0,1:T(8,128)(2,1)} dynamic-update-slice(bf16[128,11264]{0,1:T(8,128)(2,1)} %dynamic_update_slice.12, bf16[32,11264]{0,1:T(8,128)(2,1)} %copy.60, s32[]{:T(128)S(6)} %select_n.208, s32[]{:T(128)} %constant.288.clone.1) | dynamic-update-slice | bytes 1441796 | tf_op jit(solution)/shard_map/dynamic_update_slice | solution.py:19
  179.1 30.9 %dynamic_update_slice.14 = bf16[128,11264]{0,1:T(8,128)(2,1)} dynamic-update-slice(bf16[128,11264]{0,1:T(8,128)(2,1)} %dynamic_update_slice.13, bf16[32,11264]{0,1:T(8,128)(2,1)} %copy.61, s32[]{:T(128)S(6)} %select_n.210, s32[]{:T(128)} %constant.288.clone.1) | dynamic-update-slice | bytes 1441796 | tf_op jit(solution)/shard_map/dynamic_update_slice | solution.py:22
  213.8 30.9 %dynamic_update_slice.15 = bf16[128,11264]{0,1:T(8,128)(2,1)} dynamic-update-slice(bf16[128,11264]{0,1:T(8,128)(2,1)} %dynamic_update_slice.14, bf16[32,11264]{0,1:T(8,128)(2,1)} %copy.62, s32[]{:T(128)S(6)} %select_n.212, s32[]{:T(128)} %constant.288.clone.1) | dynamic-update-slice | bytes 1441796 | tf_op jit(solution)/shard_map/dynamic_update_slice | solution.py:19
  244.7 4.5 %copy.64 = bf16[128,44,256]{2,0,1:T(8,128)(2,1)} copy(bf16[128,44,256]{0,2,1:T(8,128)(2,1)} %bitcast.197) | data formatting | bytes 5767168
  249.3 96.8 %while.14 = (s32[]{:T(128)}, f32[128,8,256]{0,2,1:T(8,128)}, s32[8,12]{0,1:T(8,128)}, f32[4,20,256]{2,0,1:T(4,128)S(1)}, f32[4,8,256]{2,1,0:T(8,128)S(1)}, /*ind...) while((s32[]{:T(128)}, f32[128,8,256]{0,2,1:T(8,128)}, ...), condition=%wide.region_1.2_spmd.clone, body=%wide.region_0.1_spmd.clone.sunk | while | flops 142354592 | bytes 4072003 | solution.py:109
  259.9 4.3 %fusion.174 = f32[128,8,256]{0,2,1:T(8,128)} fusion(f32[128,8,256]{0,2,1:T(8,128)} %get-tuple-element.350, f32[8]{0:T(128)S(1)} %compare_convert_fusion.2, f32[8,256]{1,0:T(8,128)S(1)} %get-tuple-element.324, f32[8,256]{1,0:T(8,128)S(1)} %get-tuple-element.328, f32[8,256]{1,0:T(8,128)S(1)} %get-tuple-element.329, ...), kind=kOutput, calls=%fused_computation.6.clone.1 | convolution fusion | flops 142344192 | bytes 2687017 | tf_op jit(solution)/shard_map/while/body/eval_jaxpr/rcs,cts->rct/dot_general | solution.py:104
  268.1 4.3 %fusion.174 = f32[128,8,256]{0,2,1:T(8,128)} fusion(f32[128,8,256]{0,2,1:T(8,128)} %get-tuple-element.350, f32[8]{0:T(128)S(1)} %compare_convert_fusion.2, f32[8,256]{1,0:T(8,128)S(1)} %get-tuple-element.324, f32[8,256]{1,0:T(8,128)S(1)} %get-tuple-element.328, f32[8,256]{1,0:T(8,128)S(1)} %get-tuple-element.329, ...), kind=kOutput, calls=%fused_computation.6.clone.1 | convolution fusion | flops 142344192 | bytes 2687017 | tf_op jit(solution)/shard_map/while/body/eval_jaxpr/rcs,cts->rct/dot_general | solution.py:104
  276.3 4.3 %fusion.174 = f32[128,8,256]{0,2,1:T(8,128)} fusion(f32[128,8,256]{0,2,1:T(8,128)} %get-tuple-element.350, f32[8]{0:T(128)S(1)} %compare_convert_fusion.2, f32[8,256]{1,0:T(8,128)S(1)} %get-tuple-element.324, f32[8,256]{1,0:T(8,128)S(1)} %get-tuple-element.328, f32[8,256]{1,0:T(8,128)S(1)} %get-tuple-element.329, ...), kind=kOutput, calls=%fused_computation.6.clone.1 | convolution fusion | flops 142344192 | bytes 2687017 | tf_op jit(solution)/shard_map/while/body/eval_jaxpr/rcs,cts->rct/dot_general | solution.py:104
  284.5 4.3 %fusion.174 = f32[128,8,256]{0,2,1:T(8,128)} fusion(f32[128,8,256]{0,2,1:T(8,128)} %get-tuple-element.350, f32[8]{0:T(128)S(1)} %compare_convert_fusion.2, f32[8,256]{1,0:T(8,128)S(1)} %get-tuple-element.324, f32[8,256]{1,0:T(8,128)S(1)} %get-tuple-element.328, f32[8,256]{1,0:T(8,128)S(1)} %get-tuple-element.329, ...), kind=kOutput, calls=%fused_computation.6.clone.1 | convolution fusion | flops 142344192 | bytes 2687017 | tf_op jit(solution)/shard_map/while/body/eval_jaxpr/rcs,cts->rct/dot_general | solution.py:104
  292.7 4.3 %fusion.174 = f32[128,8,256]{0,2,1:T(8,128)} fusion(f32[128,8,256]{0,2,1:T(8,128)} %get-tuple-element.350, f32[8]{0:T(128)S(1)} %compare_convert_fusion.2, f32[8,256]{1,0:T(8,128)S(1)} %get-tuple-element.324, f32[8,256]{1,0:T(8,128)S(1)} %get-tuple-element.328, f32[8,256]{1,0:T(8,128)S(1)} %get-tuple-element.329, ...), kind=kOutput, calls=%fused_computation.6.clone.1 | convolution fusion | flops 142344192 | bytes 2687017 | tf_op jit(solution)/shard_map/while/body/eval_jaxpr/rcs,cts->rct/dot_general | solution.py:104
  300.8 4.3 %fusion.174 = f32[128,8,256]{0,2,1:T(8,128)} fusion(f32[128,8,256]{0,2,1:T(8,128)} %get-tuple-element.350, f32[8]{0:T(128)S(1)} %compare_convert_fusion.2, f32[8,256]{1,0:T(8,128)S(1)} %get-tuple-element.324, f32[8,256]{1,0:T(8,128)S(1)} %get-tuple-element.328, f32[8,256]{1,0:T(8,128)S(1)} %get-tuple-element.329, ...), kind=kOutput, calls=%fused_computation.6.clone.1 | convolution fusion | flops 142344192 | bytes 2687017 | tf_op jit(solution)/shard_map/while/body/eval_jaxpr/rcs,cts->rct/dot_general | solution.py:104
  309.0 4.3 %fusion.174 = f32[128,8,256]{0,2,1:T(8,128)} fusion(f32[128,8,256]{0,2,1:T(8,128)} %get-tuple-element.350, f32[8]{0:T(128)S(1)} %compare_convert_fusion.2, f32[8,256]{1,0:T(8,128)S(1)} %get-tuple-element.324, f32[8,256]{1,0:T(8,128)S(1)} %get-tuple-element.328, f32[8,256]{1,0:T(8,128)S(1)} %get-tuple-element.329, ...), kind=kOutput, calls=%fused_computation.6.clone.1 | convolution fusion | flops 142344192 | bytes 2687017 | tf_op jit(solution)/shard_map/while/body/eval_jaxpr/rcs,cts->rct/dot_general | solution.py:104
  317.2 4.3 %fusion.174 = f32[128,8,256]{0,2,1:T(8,128)} fusion(f32[128,8,256]{0,2,1:T(8,128)} %get-tuple-element.350, f32[8]{0:T(128)S(1)} %compare_convert_fusion.2, f32[8,256]{1,0:T(8,128)S(1)} %get-tuple-element.324, f32[8,256]{1,0:T(8,128)S(1)} %get-tuple-element.328, f32[8,256]{1,0:T(8,128)S(1)} %get-tuple-element.329, ...), kind=kOutput, calls=%fused_computation.6.clone.1 | convolution fusion | flops 142344192 | bytes 2687017 | tf_op jit(solution)/shard_map/while/body/eval_jaxpr/rcs,cts->rct/dot_general | solution.py:104
  325.4 4.3 %fusion.174 = f32[128,8,256]{0,2,1:T(8,128)} fusion(f32[128,8,256]{0,2,1:T(8,128)} %get-tuple-element.350, f32[8]{0:T(128)S(1)} %compare_convert_fusion.2, f32[8,256]{1,0:T(8,128)S(1)} %get-tuple-element.324, f32[8,256]{1,0:T(8,128)S(1)} %get-tuple-element.328, f32[8,256]{1,0:T(8,128)S(1)} %get-tuple-element.329, ...), kind=kOutput, calls=%fused_computation.6.clone.1 | convolution fusion | flops 142344192 | bytes 2687017 | tf_op jit(solution)/shard_map/while/body/eval_jaxpr/rcs,cts->rct/dot_general | solution.py:104
  333.6 4.3 %fusion.174 = f32[128,8,256]{0,2,1:T(8,128)} fusion(f32[128,8,256]{0,2,1:T(8,128)} %get-tuple-element.350, f32[8]{0:T(128)S(1)} %compare_convert_fusion.2, f32[8,256]{1,0:T(8,128)S(1)} %get-tuple-element.324, f32[8,256]{1,0:T(8,128)S(1)} %get-tuple-element.328, f32[8,256]{1,0:T(8,128)S(1)} %get-tuple-element.329, ...), kind=kOutput, calls=%fused_computation.6.clone.1 | convolution fusion | flops 142344192 | bytes 2687017 | tf_op jit(solution)/shard_map/while/body/eval_jaxpr/rcs,cts->rct/dot_general | solution.py:104
  341.8 4.3 %fusion.174 = f32[128,8,256]{0,2,1:T(8,128)} fusion(f32[128,8,256]{0,2,1:T(8,128)} %get-tuple-element.350, f32[8]{0:T(128)S(1)} %compare_convert_fusion.2, f32[8,256]{1,0:T(8,128)S(1)} %get-tuple-element.324, f32[8,256]{1,0:T(8,128)S(1)} %get-tuple-element.328, f32[8,256]{1,0:T(8,128)S(1)} %get-tuple-element.329, ...), kind=kOutput, calls=%fused_computation.6.clone.1 | convolution fusion | flops 142344192 | bytes 2687017 | tf_op jit(solution)/shard_map/while/body/eval_jaxpr/rcs,cts->rct/dot_general | solution.py:104
  356.0 5.1 %all-to-all-done = bf16[4,32,2048]{2,1,0:T(8,128)(2,1)} async-done(((bf16[4,32,2048]{2,1,0:T(8,128)(2,1)}), bf16[4,32,2048]{2,1,0:T(8,128)(2,1)}, u32[]{:S(2)}, u32[]{:S(2)}) %all-to-all-start) | async-done | bytes 524320 | tf_op jit(solution)/shard_map/all_to_all | solution.py:110
  (283 shorter events, 146.2 us)
Async XLA Ops:
  0.0 106.3 %copy-start = (bf16[32,4,64,64]{3,2,1,0:T(8,128)(2,1)S(1)}, bf16[32,4,64,64]{3,2,1,0:T(8,128)(2,1)}, u32[]{:S(2)}) copy-start(bf16[32,4,64,64]{3,2,1,0:T(8,128)(2,1)} %param.24) | copy-start | bytes 3145732
  2.7 24.0 %copy-start.14 = (s32[32,4]{0,1:T(4,128)S(1)}, s32[32,4]{0,1:T(4,128)}, u32[]{:S(2)}) copy-start(s32[32,4]{0,1:T(4,128)} %param.19) | copy-start | bytes 1540
  2.7 25.3 %copy-start.13 = (s32[32,12]{0,1:T(8,128)S(1)}, s32[32,12]{0,1:T(8,128)}, u32[]{:S(2)}) copy-start(s32[32,12]{0,1:T(8,128)} %param.18) | copy-start | bytes 4612
  2.7 25.9 %copy-start.7 = (bf16[2,64,64]{2,1,0:T(8,128)(2,1)S(1)}, bf16[2,64,64]{2,1,0:T(8,128)(2,1)}, u32[]{:S(2)}) copy-start(bf16[2,64,64]{2,1,0:T(8,128)(2,1)} %param.26) | copy-start | bytes 49156
  2.7 26.1 %copy-start.4 = (bf16[2,64,64]{2,1,0:T(8,128)(2,1)S(1)}, bf16[2,64,64]{2,1,0:T(8,128)(2,1)}, u32[]{:S(2)}) copy-start(bf16[2,64,64]{2,1,0:T(8,128)(2,1)} %param.25) | copy-start | bytes 49156
  2.7 78.4 %collective-permute-start.1 = (f32[36,1536]{1,0:T(8,128)}, f32[36,1536]{1,0:T(8,128)}, u32[]{:S(2)}, u32[]{:S(2)}) collective-permute-start(f32[36,1536]{1,0:T(8,128)} %get-tuple-element.255), channel_id=1, source_target_pairs={{4,0},{8,4},{12,8},{16,12},{20,16},{24,20},{28,24},{32,28},{36,32}... | collective-permute-start | bytes 663560 | tf_op jit(solution)/shard_map/ppermute | solution.py:36
  5.6 75.5 %collective-permute-start = (f32[36,1536]{1,0:T(8,128)}, f32[36,1536]{1,0:T(8,128)}, u32[]{:S(2)}, u32[]{:S(2)}) collective-permute-start(f32[36,1536]{1,0:T(8,128)} %get-tuple-element.254), channel_id=1, source_target_pairs={{0,4},{4,8},{8,12},{12,16},{16,20},{20,24},{24,28},{28,32},{32,36}... | collective-permute-start | bytes 663560 | tf_op jit(solution)/shard_map/ppermute | solution.py:35
  7.5 71.0 %copy-start.8 = (bf16[2,64,64]{2,1,0:T(8,128)(2,1)S(1)}, bf16[2,64,64]{2,1,0:T(8,128)(2,1)}, u32[]{:S(2)}) copy-start(bf16[2,64,64]{2,1,0:T(8,128)(2,1)} %param.27) | copy-start | bytes 49156
  12.7 91.5 %collective-permute-start.6 = (bf16[32,512]{1,0:T(8,128)(2,1)}, bf16[32,512]{1,0:T(8,128)(2,1)}, u32[]{:S(2)}, u32[]{:S(2)}) collective-permute-start(bf16[32,512]{1,0:T(8,128)(2,1)} %get-tuple-element.259), channel_id=1, source_target_pairs={{4,0},{8,4},{12,8},{16,12},{20,16},{24,20},{28,24},{32,28},{36,32}... | collective-permute-start | bytes 98312 | tf_op jit(solution)/shard_map/ppermute | solution.py:36
  16.3 87.9 %collective-permute-start.5 = (bf16[32,512]{1,0:T(8,128)(2,1)}, bf16[32,512]{1,0:T(8,128)(2,1)}, u32[]{:S(2)}, u32[]{:S(2)}) collective-permute-start(bf16[32,512]{1,0:T(8,128)(2,1)} %get-tuple-element.258), channel_id=1, source_target_pairs={{0,4},{4,8},{8,12},{12,16},{16,20},{20,24},{24,28},{28,32},{32,36}... | collective-permute-start | bytes 98312 | tf_op jit(solution)/shard_map/ppermute | solution.py:35
  20.8 8.1 %collective-permute-start.7 = (bf16[32,64]{1,0:T(8,128)(2,1)S(1)}, bf16[32,64]{1,0:T(8,128)(2,1)S(1)}, u32[]{:S(2)}, u32[]{:S(2)}) collective-permute-start(bf16[32,64]{1,0:T(8,128)(2,1)S(1)} %fusion.23), channel_id=1, source_target_pairs={{0,4},{4,0},{8,12},{12,8},{16,20},{20,16},{24,28},{28,24},{32,36},... | collective-permute-start | bytes 12296 | tf_op jit(solution)/shard_map/ppermute | solution.py:42
  28.9 53.4 %copy-start.10 = (bf16[32,64]{1,0:T(8,128)(2,1)}, bf16[32,64]{1,0:T(8,128)(2,1)S(1)}, u32[]{:S(2)}) copy-start(bf16[32,64]{1,0:T(8,128)(2,1)S(1)} %collective-permute-done.7) | copy-start | bytes 12292
  29.1 5.5 %collective-permute-start.8 = (bf16[32,64]{1,0:T(8,128)(2,1)S(1)}, bf16[32,64]{1,0:T(8,128)(2,1)S(1)}, u32[]{:S(2)}, u32[]{:S(2)}) collective-permute-start(bf16[32,64]{1,0:T(8,128)(2,1)S(1)} %fusion.24), channel_id=1, source_target_pairs={{0,8},{4,12},{8,0},{12,4},{16,24},{20,28},{24,16},{28,20},{32,40},... | collective-permute-start | bytes 12296 | tf_op jit(solution)/shard_map/ppermute | solution.py:42
  34.7 6.4 %collective-permute-start.9 = (bf16[32,64]{1,0:T(8,128)(2,1)S(1)}, bf16[32,64]{1,0:T(8,128)(2,1)S(1)}, u32[]{:S(2)}, u32[]{:S(2)}) collective-permute-start(bf16[32,64]{1,0:T(8,128)(2,1)S(1)} %fusion.25), channel_id=1, source_target_pairs={{0,16},{4,20},{8,24},{12,28},{16,0},{20,4},{24,8},{28,12},{32,48},... | collective-permute-start | bytes 12296 | tf_op jit(solution)/shard_map/ppermute | solution.py:42
  41.3 9.4 %collective-permute-start.10 = (bf16[32,64]{1,0:T(8,128)(2,1)S(1)}, bf16[32,64]{1,0:T(8,128)(2,1)S(1)}, u32[]{:S(2)}, u32[]{:S(2)}) collective-permute-start(bf16[32,64]{1,0:T(8,128)(2,1)S(1)} %fusion.26), channel_id=1, source_target_pairs={{0,32},{4,36},{8,40},{12,44},{16,48},{20,52},{24,56},{28,60},{32,0... | collective-permute-start | bytes 12296 | tf_op jit(solution)/shard_map/ppermute | solution.py:42
  50.9 5.9 %collective-permute-start.11 = (bf16[32,64]{1,0:T(8,128)(2,1)S(1)}, bf16[32,64]{1,0:T(8,128)(2,1)S(1)}, u32[]{:S(2)}, u32[]{:S(2)}) collective-permute-start(bf16[32,64]{1,0:T(8,128)(2,1)S(1)} %fusion.27), channel_id=1, source_target_pairs={{0,64},{4,68},{8,72},{12,76},{16,80},{20,84},{24,88},{28,92},{32,9... | collective-permute-start | bytes 12296 | tf_op jit(solution)/shard_map/ppermute | solution.py:42
  56.8 11.0 %copy-start.11 = (bf16[32,64]{1,0:T(8,128)(2,1)}, bf16[32,64]{1,0:T(8,128)(2,1)S(1)}, u32[]{:S(2)}) copy-start(bf16[32,64]{1,0:T(8,128)(2,1)S(1)} %collective-permute-done.11) | copy-start | bytes 12292
  56.9 10.1 %collective-permute-start.12 = (bf16[32,64]{1,0:T(8,128)(2,1)S(1)}, bf16[32,64]{1,0:T(8,128)(2,1)S(1)}, u32[]{:S(2)}, u32[]{:S(2)}) collective-permute-start(bf16[32,64]{1,0:T(8,128)(2,1)S(1)} %fusion.28), channel_id=1, source_target_pairs={{0,128},{4,132},{8,136},{12,140},{16,144},{20,148},{24,152},{28,15... | collective-permute-start | bytes 12296 | tf_op jit(solution)/shard_map/ppermute | solution.py:42
  67.8 10.7 %collective-permute-start.13 = (bf16[32,64]{1,0:T(8,128)(2,1)}, bf16[32,64]{1,0:T(8,128)(2,1)S(1)}, u32[]{:S(2)}, u32[]{:S(2)}) collective-permute-start(bf16[32,64]{1,0:T(8,128)(2,1)} %fusion.29), channel_id=1, source_target_pairs={{0,256},{4,260},{8,264},{12,268},{16,272},{20,276},{24,280},{28,28... | collective-permute-start | bytes 12296 | tf_op jit(solution)/shard_map/ppermute | solution.py:42
  81.1 23.2 %copy-start.6 = (bf16[32,2048]{1,0:T(8,128)(2,1)S(1)}, bf16[32,2048]{1,0:T(8,128)(2,1)}, u32[]{:S(2)}) copy-start(bf16[32,2048]{1,0:T(8,128)(2,1)} %reshape.114) | copy-start | bytes 393220
  84.5 16.3 %collective-permute-start.2 = (bf16[32,11264]{1,0:T(8,128)(2,1)}, bf16[32,11264]{1,0:T(8,128)(2,1)}, u32[]{:S(2)}, u32[]{:S(2)}) collective-permute-start(bf16[32,11264]{1,0:T(8,128)(2,1)} %slice.115), channel_id=1, source_target_pairs={{0,1},{1,2},{2,3},{3,0},{4,5},{5,6},{6,7},{7,4},{8,9},{9,10},{10,1... | collective-permute-start | bytes 2162696 | tf_op jit(solution)/shard_map/ppermute | solution.py:18
  89.2 86.1 %collective-permute-start.3 = (bf16[32,11264]{1,0:T(8,128)(2,1)}, bf16[32,11264]{1,0:T(8,128)(2,1)}, u32[]{:S(2)}, u32[]{:S(2)}) collective-permute-start(bf16[32,11264]{1,0:T(8,128)(2,1)} %slice.115), channel_id=1, source_target_pairs={{0,3},{1,0},{2,1},{3,2},{4,7},{5,4},{6,5},{7,6},{8,11},{9,8},{10,9... | collective-permute-start | bytes 2162696 | tf_op jit(solution)/shard_map/ppermute | solution.py:21
  100.9 109.2 %collective-permute-start.4 = (bf16[32,11264]{1,0:T(8,128)(2,1)}, bf16[32,11264]{1,0:T(8,128)(2,1)}, u32[]{:S(2)}, u32[]{:S(2)}) collective-permute-start(bf16[32,11264]{1,0:T(8,128)(2,1)} %collective-permute-done.2), channel_id=1, source_target_pairs={{0,1},{1,2},{2,3},{3,0},{4,5},{5,6},{6,7},{7,4},{8,9},{9,10},{10,1... | collective-permute-start | bytes 2162696 | tf_op jit(solution)/shard_map/ppermute | solution.py:18
  348.9 12.3 %all-to-all-start = ((bf16[4,32,2048]{2,1,0:T(8,128)(2,1)}), bf16[4,32,2048]{2,1,0:T(8,128)(2,1)}, u32[]{:S(2)}, u32[]{:S(2)}) async-start(bf16[4,32,2048]{2,1,0:T(8,128)(2,1)} %convert_element_type.77), calls=%async_computation | async-start | bytes 1048576 | tf_op jit(solution)/shard_map/all_to_all | solution.py:110
  (8 other events, 32.4 us)
